TPU v7x, 512 devices: a whole 4x4x16 slice. The times are simulated.
512 devices in a mesh: gx: 64 (over y, z), ta: 8 (over x, core).
Axes of the slice: x: 4, y: 4, z: 16, core: 2. Of those that a mesh axis runs over, the one named last changes fastest.
Arguments:
- query_vecs: bfloat16 [256, 64, 5120], P('gx', None, 'ta'), may hold values from -32 to 32
- key_vecs: bfloat16 [256, 64, 5120], P('gx', None, 'ta'), may hold values from -6 to 6
- value_vecs: bfloat16 [256, 64, 5120], P('gx', None, 'ta'), may hold values from -6 to 6
- slot_map: int32 [16, 64], replicated, may hold values from 0 to 63, each once within a row
- edge_list: int32 [256, 2], replicated, may hold values from 0 to 63
- edge_types: int32 [256], replicated, may hold values from 0 to 2
- type_gain: float32 [2, 3, 5120], P(None, None, 'ta'), may hold values from 0.25 to 2
- norm_gain: float32 [2, 5120], P(None, 'ta'), may hold values from 0.5 to 2
- gate_proj: bfloat16 [2, 5120, 20480], P(None, 'ta', 'gx'), may hold values from -0.078125 to 0.078125
- up_proj: bfloat16 [2, 5120, 20480], P(None, 'ta', 'gx'), may hold values from -0.078125 to 0.078125
- down_proj: bfloat16 [2, 20480, 5120], P(None, 'gx', 'ta'), may hold values from -0.0390625 to 0.0390625
Outputs:
- node_states: bfloat16 [512, 5120], P('gx', 'ta')
All inputs are finite; a program needn't handle non-finite values.
Results may differ from a plain program's by a relative error of at most 0.04.
Values may be sent and summed in bfloat16 or wider, within the bound.
A program may use at most 64 MiB of HBM per device.

v0:
```python
import jax
import jax.numpy as jnp
from jax import lax
from jax.sharding import PartitionSpec as P

D = 5120
HEAD_DIM = 128
VENUES = 16
STEPS = 16
NODE_STEPS = 8
ROUNDS = 2
ETYPES = 3


def settle_rows(nodes, hidden, down_local, row_begin, rows_dev):
    summed = lax.psum_scatter(
        jnp.dot(hidden, down_local, preferred_element_type=jnp.float32),
        "gx",
        scatter_dimension=0,
        tiled=True,
    )
    base_rows = lax.dynamic_slice_in_dim(nodes, row_begin, rows_dev, 0)
    return (base_rows.astype(jnp.float32) + summed).astype(jnp.bfloat16)


def per_device(
    query_vecs,
    key_vecs,
    value_vecs,
    slot_map,
    edge_list,
    edge_types,
    type_gain,
    norm_gain,
    gate_proj,
    up_proj,
    down_proj,
):
    pairs_dev = query_vecs.shape[0]
    inst_total = query_vecs.shape[1]
    feat_width = query_vecs.shape[2]
    head_count = feat_width // HEAD_DIM
    gx_count = lax.axis_size("gx")
    inst_local = inst_total // gx_count
    score_scale = 1.0 / HEAD_DIM**0.5
    venue_idx = lax.axis_index("gx") * pairs_dev // STEPS
    slot_order = lax.dynamic_index_in_dim(slot_map, venue_idx, 0, keepdims=False)
    split_shape = (pairs_dev, gx_count, inst_local, feat_width)
    sorted_queries = jnp.take(query_vecs, slot_order, axis=1).reshape(split_shape)
    sorted_keys = jnp.take(key_vecs, slot_order, axis=1).reshape(split_shape)
    sorted_values = jnp.take(value_vecs, slot_order, axis=1).reshape(split_shape)
    query_steps = jnp.arange(VENUES * NODE_STEPS) % NODE_STEPS + (STEPS - NODE_STEPS)
    key_steps = jnp.arange(VENUES * STEPS) % STEPS
    allowed = key_steps[None, :] <= query_steps[:, None]
    queries = lax.all_to_all(sorted_queries, "gx", split_axis=1, concat_axis=0, tiled=True)
    keyset = lax.all_to_all(sorted_keys, "gx", split_axis=1, concat_axis=0, tiled=True)
    valueset = lax.all_to_all(sorted_values, "gx", split_axis=1, concat_axis=0, tiled=True)
    pair_total = queries.shape[0]
    item_count = queries.shape[2]
    queries = queries.reshape(VENUES, STEPS, item_count, head_count, HEAD_DIM)[
        :, STEPS - NODE_STEPS :
    ]
    queries = queries.reshape(VENUES * NODE_STEPS, item_count, head_count, HEAD_DIM)
    keyset = keyset.reshape(pair_total, item_count, head_count, HEAD_DIM)
    valueset = valueset.reshape(pair_total, item_count, head_count, HEAD_DIM)
    scores = (
        jnp.einsum("qnhd,knhd->nhqk", queries, keyset, preferred_element_type=jnp.float32)
        * score_scale
    )
    scores = jnp.where(allowed[None, None], scores, jnp.float32(-1e30))
    row_max = jnp.max(scores, axis=-1, keepdims=True)
    expd = jnp.exp(scores - row_max)
    probs = (expd / jnp.sum(expd, axis=-1, keepdims=True)).astype(jnp.bfloat16)
    attended = jnp.einsum("nhqk,knhd->nqhd", probs, valueset, preferred_element_type=jnp.float32)
    attended = attended.reshape(item_count, VENUES, NODE_STEPS, feat_width)
    pooled = jnp.mean(attended, axis=1).astype(jnp.bfloat16)
    own_rows = pooled.reshape(inst_local * NODE_STEPS, feat_width)
    rows_dev = own_rows.shape[0]
    row_begin = lax.axis_index("gx") * rows_dev
    nodes = lax.all_gather(own_rows, "gx", axis=0, tiled=True)
    row_total = nodes.shape[0]
    node_ids = jnp.arange(inst_total)
    type_ids = jnp.arange(ETYPES)
    at_source = (edge_list[:, 0][:, None] == node_ids[None, :]).astype(jnp.float32)
    at_target = (edge_list[:, 1][:, None] == node_ids[None, :]).astype(jnp.float32)
    of_type = (edge_types[:, None] == type_ids[None, :]).astype(jnp.float32)
    adjacency = jnp.einsum("et,ei,ej->tij", of_type, at_target, at_source)
    degree = jnp.maximum(jnp.sum(at_target, axis=0), 1.0)
    adj_rows = adjacency.reshape(ETYPES * inst_total, inst_total).astype(jnp.bfloat16)
    for layer_idx in range(ROUNDS):
        flat_nodes = nodes.reshape(inst_total, NODE_STEPS * feat_width)
        gathered = jnp.dot(adj_rows, flat_nodes, preferred_element_type=jnp.float32)
        gathered = gathered.reshape(ETYPES, inst_total, NODE_STEPS, feat_width)
        message = (
            jnp.sum(gathered * type_gain[layer_idx][:, None, None, :], axis=0)
            / degree[:, None, None]
        )
        pre_norm = nodes.astype(jnp.float32) + message.reshape(row_total, feat_width)
        squares = lax.psum(jnp.sum(pre_norm * pre_norm, axis=-1), "ta")
        row_scale = lax.rsqrt(squares / D + 1e-05)[:, None]
        normed = (pre_norm * row_scale * norm_gain[layer_idx][None, :]).astype(jnp.bfloat16)
        gate_part = jnp.dot(normed, gate_proj[layer_idx], preferred_element_type=jnp.float32)
        up_part = jnp.dot(normed, up_proj[layer_idx], preferred_element_type=jnp.float32)
        gate_sum, up_sum = (
            lax.psum(gate_part.astype(jnp.bfloat16), "ta").astype(jnp.float32),
            lax.psum(up_part.astype(jnp.bfloat16), "ta").astype(jnp.float32),
        )
        hidden = (jax.nn.silu(gate_sum) * up_sum).astype(jnp.bfloat16)
        down_local = down_proj[layer_idx]
        if layer_idx == ROUNDS - 1:
            own_rows = settle_rows(nodes, hidden, down_local, row_begin, rows_dev)
        else:
            own_rows = settle_rows(nodes, hidden, down_local, row_begin, rows_dev)
            nodes = lax.all_gather(own_rows, "gx", axis=0, tiled=True)
    return own_rows


def solution(mesh):
    placed = (
        P("gx", None, "ta"),
        P("gx", None, "ta"),
        P("gx", None, "ta"),
        P(),
        P(),
        P(),
        P(None, None, "ta"),
        P(None, "ta"),
        P(None, "ta", "gx"),
        P(None, "ta", "gx"),
        P(None, "gx", "ta"),
    )
    return jax.shard_map(
        per_device, mesh=mesh, in_specs=placed, out_specs=P("gx", "ta"), check_vma=False
    )
```

profile of v0, /device:TPU:2, one launch (start us, length us, event | category | flops | bytes accessed | tf_op | source)
XLA Modules:
  0.0 1049.3 jit_solution(5708310502350677954)
XLA Ops:
  7.5 1.6 gather_fusion
  9.1 1.6 gather_fusion.1
  10.8 1.6 gather_fusion.2
  13.5 18.9 %all-to-all-start.1 = ((bf16[4,64,1,640]{3,0,2,1:T(4,128)(2,1)}), bf16[4,64,1,640]{3,0,2,1:T(4,128)(2,1)S(1)}, u32[]{:S(2)}, u32[]{:S(2)}) async-start(bf16[4,64,1,640]{3,0,2,1:T(4,128)(2,1)} %copy.32), calls=%async_computation.1 | async-start | bytes 655360 | tf_op jit(solution)/shard_map/all_to_all | solution.py:55
  33.4 22.7 %all-to-all-done.1 = bf16[4,64,1,640]{3,0,2,1:T(4,128)(2,1)S(1)} async-done(((bf16[4,64,1,640]{3,0,2,1:T(4,128)(2,1)}), bf16[4,64,1,640]{3,0,2,1:T(4,128)(2,1)S(1)}, u32[]{:S(2)}, u32[]{:S(2)}) %all-to-all-start.1) | async-done | bytes 327712 | tf_op jit(solution)/shard_map/all_to_all | solution.py:55
  56.1 6.5 all-to-all-start.2
  64.0 21.6 %all-to-all-done.2 = bf16[4,64,1,640]{3,0,2,1:T(4,128)(2,1)S(1)} async-done(((bf16[4,64,1,640]{3,0,2,1:T(4,128)(2,1)}), bf16[4,64,1,640]{3,0,2,1:T(4,128)(2,1)S(1)}, u32[]{:S(2)}, u32[]{:S(2)}) %all-to-all-start.2) | async-done | bytes 327712 | tf_op jit(solution)/shard_map/all_to_all | solution.py:56
  85.6 6.6 all-to-all-start
  93.6 20.9 %all-to-all-done = bf16[4,64,1,640]{3,0,2,1:T(4,128)(2,1)S(1)} async-done(((bf16[4,64,1,640]{3,0,2,1:T(4,128)(2,1)}), bf16[4,64,1,640]{3,0,2,1:T(4,128)(2,1)S(1)}, u32[]{:S(2)}, u32[]{:S(2)}) %all-to-all-start) | async-done | bytes 327712 | tf_op jit(solution)/shard_map/all_to_all | solution.py:57
  114.6 1.4 convolution_bitcast_fusion
  116.4 99.8 %all_gather.6 = bf16[512,640]{1,0:T(8,128)(2,1)S(1)} all-gather(bf16[8,640]{1,0:T(8,128)(2,1)S(1)} %multiply_convert_fusion.2), channel_id=1, replica_groups=mesh['gx'=64,'ta'=8] {'gx'}, dimensions={0}, use_global_device_ids=true | all-gather | bytes 665600 | tf_op jit(solution)/shard_map/all_gather | solution.py:80
  218.1 10.0 psum.42
  228.1 1.3 convolution_convert_fusion.3
  230.7 67.0 %all-reduce.15.cloned.1.call-done = (bf16[512,320]{0,1:T(8,128)(2,1)}, bf16[512,320]{0,1:T(8,128)(2,1)}) async-done(((bf16[512,320]{0,1:T(8,128)(2,1)}, bf16[512,320]{0,1:T(8,128)(2,1)}), (bf16[512,320]{0,1:T(8,128)(2,1)}, bf16[512,320]{0,1:T(8,128)(2,1)})) %all-reduce.15.cloned.1.call-update) | async-done | bytes 655376 | tf_op jit(solution)/shard_map/psum | solution.py:106
  297.7 2.9 fusion.23
  300.7 1.3 dynamic-slice
  302.6 275.2 %all-reduce.9.cloned.1.call-done = f32[512,640]{1,0:T(8,128)} async-done(((f32[512,640]{1,0:T(8,128)}), f32[512,640]{1,0:T(8,128)}) %all-reduce.9.cloned.1.call-update) | async-done | bytes 1310736
  578.6 98.7 %all_gather.7 = bf16[512,640]{1,0:T(8,128)(2,1)S(1)} all-gather(bf16[8,640]{1,0:T(8,128)(2,1)S(1)} %fusion.51), channel_id=1, replica_groups=mesh['gx'=64,'ta'=8] {'gx'}, dimensions={0}, use_global_device_ids=true | all-gather | bytes 665600 | tf_op jit(solution)/shard_map/all_gather | solution.py:114
  679.2 10.0 psum.45
  689.2 1.3 convolution_convert_fusion.1
  691.8 69.7 %all-reduce.13.cloned.1.call-done = (bf16[512,320]{0,1:T(8,128)(2,1)}, bf16[512,320]{0,1:T(8,128)(2,1)}) async-done(((bf16[512,320]{0,1:T(8,128)(2,1)}, bf16[512,320]{0,1:T(8,128)(2,1)}), (bf16[512,320]{0,1:T(8,128)(2,1)}, bf16[512,320]{0,1:T(8,128)(2,1)})) %all-reduce.13.cloned.1.call-update) | async-done | bytes 655376 | tf_op jit(solution)/shard_map/psum | solution.py:106
  761.5 2.8 fusion.19
  764.3 277.2 %all-reduce.11.cloned.1.call-done = f32[512,640]{1,0:T(8,128)} async-done(((f32[512,640]{1,0:T(8,128)}), f32[512,640]{1,0:T(8,128)}) %all-reduce.11.cloned.1.call-update) | async-done | bytes 1310736
  1041.4 1.3 fusion.50
  (72 shorter events, 13.5 us)
Async XLA Ops:
  6.5 1.0 copy-start
  7.5 1.6 copy-start.1
  9.1 1.6 copy-start.2
  13.5 50.0 %copy-start.6 = (f32[2,3,640]{2,0,1:T(2,128)S(1)}, f32[2,3,640]{2,0,1:T(2,128)}, u32[]{:S(2)}) copy-start(f32[2,3,640]{2,0,1:T(2,128)} %param.19) | copy-start | bytes 46084
  13.5 50.1 %copy-start.8 = (s32[256,2]{0,1:T(2,128)S(1)}, s32[256,2]{0,1:T(2,128)}, u32[]{:S(2)}) copy-start(s32[256,2]{0,1:T(2,128)} %param.17) | copy-start | bytes 6148
  13.5 50.4 %copy-start.7 = (f32[2,640]{1,0:T(2,128)S(1)}, f32[2,640]{1,0:T(2,128)}, u32[]{:S(2)}) copy-start(f32[2,640]{1,0:T(2,128)} %param.20) | copy-start | bytes 15364
  13.5 42.6 %all-to-all-start.1 = ((bf16[4,64,1,640]{3,0,2,1:T(4,128)(2,1)}), bf16[4,64,1,640]{3,0,2,1:T(4,128)(2,1)S(1)}, u32[]{:S(2)}, u32[]{:S(2)}) async-start(bf16[4,64,1,640]{3,0,2,1:T(4,128)(2,1)} %copy.32), calls=%async_computation.1 | async-start | bytes 655360 | tf_op jit(solution)/shard_map/all_to_all | solution.py:55
  32.4 59.8 %copy-start.9 = (s32[256]{0:T(256)S(1)}, s32[256]{0:T(256)}, u32[]{:S(2)}) copy-start(s32[256]{0:T(256)} %param.18) | copy-start | bytes 3076
  56.1 29.5 %all-to-all-start.2 = ((bf16[4,64,1,640]{3,0,2,1:T(4,128)(2,1)}), bf16[4,64,1,640]{3,0,2,1:T(4,128)(2,1)S(1)}, u32[]{:S(2)}, u32[]{:S(2)}) async-start(bf16[4,64,1,640]{3,0,2,1:T(4,128)(2,1)} %copy.34), calls=%async_computation.2 | async-start | bytes 655360 | tf_op jit(solution)/shard_map/all_to_all | solution.py:56
  85.6 28.9 %all-to-all-start = ((bf16[4,64,1,640]{3,0,2,1:T(4,128)(2,1)}), bf16[4,64,1,640]{3,0,2,1:T(4,128)(2,1)S(1)}, u32[]{:S(2)}, u32[]{:S(2)}) async-start(bf16[4,64,1,640]{3,0,2,1:T(4,128)(2,1)} %copy.31), calls=%async_computation | async-start | bytes 655360 | tf_op jit(solution)/shard_map/all_to_all | solution.py:57
  92.1 205.6 %all-reduce.15.cloned.1.call-start = ((), (), s32[]{:S(2)}) async-start(), calls=%async_computation.6 | async-start | bytes 1310720 | tf_op jit(solution)/shard_map/psum | solution.py:106
  217.2 10.9 %copy-start.3 = (bf16[2,640,320]{1,2,0:T(8,128)(2,1)S(1)}, bf16[2,640,320]{1,2,0:T(8,128)(2,1)}, u32[]{:S(2)}) copy-start(bf16[2,640,320]{1,2,0:T(8,128)(2,1)} %param.21) | copy-start | bytes 2457604
  228.1 1.3 copy-start.4
  230.7 347.1 %all-reduce.9.cloned.1.call-start = ((), (), s32[]{:S(2)}) async-start(), calls=%async_computation.3 | async-start | bytes 2621440
  300.6 460.8 %all-reduce.13.cloned.1.call-start = ((), (), s32[]{:S(2)}) async-start(), calls=%async_computation.5 | async-start | bytes 1310720 | tf_op jit(solution)/shard_map/psum | solution.py:106
  689.2 1.3 copy-start.5
  690.5 71.0 %copy-start.10 = (bf16[2,320,640]{2,1,0:T(8,128)(2,1)S(1)}, bf16[2,320,640]{2,1,0:T(8,128)(2,1)}, u32[]{:S(2)}) copy-start(bf16[2,320,640]{2,1,0:T(8,128)(2,1)} %param.23) | copy-start | bytes 2457604
  691.7 349.7 %all-reduce.11.cloned.1.call-start = ((), (), s32[]{:S(2)}) async-start(), calls=%async_computation.4 | async-start | bytes 2621440
Sparse Core Ops, SparseCore 0:
  230.8 66.8 all-reduce.14
  301.1 276.7 all-reduce.8
  691.8 69.5 all-reduce.12
  764.6 276.7 all-reduce.10
where the time goes:
time: 1050 us
  waiting for transfers between devices  754 us (72%)
  blocking collectives  219 us (21%)
  starting transfers between devices  32.1 us (3%)
  matrix products  14.3 us (1%)
  between operations  14.1 us (1%)
  local copies, waits for them, and re-layouts  10.9 us (1%)
    unnamed x6, waiting for transfers between devices  552 us
    all_gather x2, blocking collectives, per_device(): nodes = lax.all_gather(own_rows, 'gx', axis=0, tiled=True)  199 us
    psum x2, waiting for transfers between devices, per_device(): lax.psum(up_part.astype(jnp.bfloat16), 'ta').astype(jnp.float32)  137 us
    all_to_all x1, waiting for transfers between devices, per_device(): lax.all_to_all(sorted_queries, 'gx', split_axis=1, concat_axis=0, tiled=T...  22.7 us
    all_to_all x1, waiting for transfers between devices, per_device(): lax.all_to_all(sorted_keys, 'gx', split_axis=1, concat_axis=0, tiled=True)  21.6 us
  transfers between devices with their start and end apart: 7, of which 7 were waited for; matrix products, arithmetic and copies ran while one was open for 0% of the time, Pallas kernels for 0%

commit v1 on v0

--- a/solution.py
+++ b/solution.py
@@ -111,7 +111,9 @@
             own_rows = settle_rows(nodes, hidden, down_local, row_begin, rows_dev)
         else:
             own_rows = settle_rows(nodes, hidden, down_local, row_begin, rows_dev)
-            nodes = lax.all_gather(own_rows, "gx", axis=0, tiled=True)
+            nodes = jnp.concatenate(
+                lax.all_to_all(jnp.stack([own_rows] * lax.axis_size("gx")), "gx", 0, 0), axis=0
+            )
     return own_rows
 
 

time: 1050 us -> 987 us (0.940)
  blocking collectives: 219 us -> 120 us
  waiting for transfers between devices: 754 us -> 779 us
    all_gather x2 -> x1, blocking collectives: 199 us -> 99.8 us  [per_device(): nodes = lax.all_gather(own_rows, 'gx', axis=0, tiled=True)]
    all_to_all x0 -> x1, waiting for transfers between devices: none -> 26.7 us  [per_device(): lax.all_to_all(jnp.stack([own_rows] * lax.axis_size('gx')), 'gx', 0, 0)]
  transfers between devices with their start and end apart: 7 -> 8, of which waited for: 7 -> 8; matrix products, arithmetic and copies ran while one was open for 0% -> 0% of each run, Pallas kernels for 0% -> 0%
where the time goes in v1:
time: 987 us
  waiting for transfers between devices  779 us (79%)
  blocking collectives  120 us (12%)
  starting transfers between devices  41.3 us (4%)
  matrix products  15.5 us (2%)
  between operations  14.1 us (1%)
  local copies, waits for them, and re-layouts  11.8 us (1%)
    unnamed x6, waiting for transfers between devices  553 us
    psum x2, waiting for transfers between devices, per_device(): lax.psum(up_part.astype(jnp.bfloat16), 'ta').astype(jnp.float32)  135 us
    all_gather x1, blocking collectives, per_device(): nodes = lax.all_gather(own_rows, 'gx', axis=0, tiled=True)  99.8 us
    all_to_all x1, waiting for transfers between devices, per_device(): lax.all_to_all(jnp.stack([own_rows] * lax.axis_size('gx')), 'gx', 0, 0)  26.7 us
    all_to_all x1, waiting for transfers between devices, per_device(): lax.all_to_all(sorted_queries, 'gx', split_axis=1, concat_axis=0, tiled=T...  22.7 us
    all_to_all x1, waiting for transfers between devices, per_device(): lax.all_to_all(sorted_keys, 'gx', split_axis=1, concat_axis=0, tiled=True)  21.6 us
    all_to_all x1, waiting for transfers between devices, per_device(): lax.all_to_all(sorted_values, 'gx', split_axis=1, concat_axis=0, tiled=True)  20.9 us
    psum x2, blocking collectives, per_device(): squares = lax.psum(jnp.sum(pre_norm * pre_norm, axis=-1), 'ta')  20.1 us
  transfers between devices with their start and end apart: 8, of which 8 were waited for; matrix products, arithmetic and copies ran while one was open for 0% of the time, Pallas kernels for 0%

profile of v1, /device:TPU:2, one launch (start us, length us, event | category | flops | bytes accessed | tf_op | source)
XLA Modules:
  0.0 986.6 jit_solution(6853408950278894890)
XLA Ops:
  7.5 1.6 gather_fusion
  9.1 1.6 gather_fusion.1
  10.8 1.6 gather_fusion.2
  13.6 18.9 %all-to-all-start.1 = ((bf16[4,64,1,640]{3,0,2,1:T(4,128)(2,1)}), bf16[4,64,1,640]{3,0,2,1:T(4,128)(2,1)S(1)}, u32[]{:S(2)}, u32[]{:S(2)}) async-start(bf16[4,64,1,640]{3,0,2,1:T(4,128)(2,1)} %copy.47), calls=%async_computation.1 | async-start | bytes 655360 | tf_op jit(solution)/shard_map/all_to_all | solution.py:55
  33.4 22.7 %all-to-all-done.1 = bf16[4,64,1,640]{3,0,2,1:T(4,128)(2,1)S(1)} async-done(((bf16[4,64,1,640]{3,0,2,1:T(4,128)(2,1)}), bf16[4,64,1,640]{3,0,2,1:T(4,128)(2,1)S(1)}, u32[]{:S(2)}, u32[]{:S(2)}) %all-to-all-start.1) | async-done | bytes 327712 | tf_op jit(solution)/shard_map/all_to_all | solution.py:55
  56.1 6.5 all-to-all-start.2
  64.0 21.6 %all-to-all-done.2 = bf16[4,64,1,640]{3,0,2,1:T(4,128)(2,1)S(1)} async-done(((bf16[4,64,1,640]{3,0,2,1:T(4,128)(2,1)}), bf16[4,64,1,640]{3,0,2,1:T(4,128)(2,1)S(1)}, u32[]{:S(2)}, u32[]{:S(2)}) %all-to-all-start.2) | async-done | bytes 327712 | tf_op jit(solution)/shard_map/all_to_all | solution.py:56
  85.6 6.6 all-to-all-start
  93.6 20.9 %all-to-all-done = bf16[4,64,1,640]{3,0,2,1:T(4,128)(2,1)S(1)} async-done(((bf16[4,64,1,640]{3,0,2,1:T(4,128)(2,1)}), bf16[4,64,1,640]{3,0,2,1:T(4,128)(2,1)S(1)}, u32[]{:S(2)}, u32[]{:S(2)}) %all-to-all-start) | async-done | bytes 327712 | tf_op jit(solution)/shard_map/all_to_all | solution.py:57
  114.7 1.4 convolution_bitcast_fusion
  116.4 99.8 %all_gather.3 = bf16[512,640]{1,0:T(8,128)(2,1)S(1)} all-gather(bf16[8,640]{1,0:T(8,128)(2,1)S(1)} %multiply_convert_fusion.2), channel_id=1, replica_groups=mesh['gx'=64,'ta'=8] {'gx'}, dimensions={0}, use_global_device_ids=true | all-gather | bytes 665600 | tf_op jit(solution)/shard_map/all_gather | solution.py:80
  218.1 10.1 %psum.42 = f32[512]{0:T(512)S(1)} all-reduce(f32[512]{0:T(512)S(1)} %get-tuple-element.12), channel_id=1, replica_groups=mesh['gx'=64,'ta'=8] {'ta'}, use_global_device_ids=true, to_apply=%region_6.8 | all-reduce | flops 512 | bytes 4096 | tf_op jit(solution)/shard_map/psum | solution.py:99
  228.3 2.3 convolution_convert_fusion.3
  231.9 67.0 %all-reduce.15.cloned.1.call-done = (bf16[512,320]{0,1:T(8,128)(2,1)}, bf16[512,320]{0,1:T(8,128)(2,1)}) async-done(((bf16[512,320]{0,1:T(8,128)(2,1)}, bf16[512,320]{0,1:T(8,128)(2,1)}), (bf16[512,320]{0,1:T(8,128)(2,1)}, bf16[512,320]{0,1:T(8,128)(2,1)})) %all-reduce.15.cloned.1.call-update) | async-done | bytes 655376 | tf_op jit(solution)/shard_map/psum | solution.py:106
  298.9 2.9 fusion.26
  303.7 275.3 %all-reduce.9.cloned.1.call-done = f32[512,640]{1,0:T(8,128)} async-done(((f32[512,640]{1,0:T(8,128)}), f32[512,640]{1,0:T(8,128)}) %all-reduce.9.cloned.1.call-update) | async-done | bytes 1310736
  580.6 9.2 all-to-all-start.3
  589.9 26.7 %all-to-all-done.3 = bf16[64,8,640]{2,1,0:T(8,128)(2,1)S(1)} async-done(((bf16[64,8,640]{2,1,0:T(8,128)(2,1)}), bf16[64,8,640]{2,1,0:T(8,128)(2,1)S(1)}, u32[]{:S(2)}, u32[]{:S(2)}) %all-to-all-start.3) | async-done | bytes 655392 | tf_op jit(solution)/shard_map/all_to_all | solution.py:115
  617.8 10.0 %psum.45 = f32[512]{0:T(512)S(1)} all-reduce(f32[512]{0:T(512)S(1)} %reduce_sum.75), channel_id=1, replica_groups=mesh['gx'=64,'ta'=8] {'ta'}, use_global_device_ids=true, to_apply=%region_12.14 | all-reduce | flops 512 | bytes 4096 | tf_op jit(solution)/shard_map/psum | solution.py:99
  629.6 1.3 convolution_convert_fusion.1
  631.0 67.7 %all-reduce.13.cloned.1.call-done = (bf16[512,320]{0,1:T(8,128)(2,1)}, bf16[512,320]{0,1:T(8,128)(2,1)}) async-done(((bf16[512,320]{0,1:T(8,128)(2,1)}, bf16[512,320]{0,1:T(8,128)(2,1)}), (bf16[512,320]{0,1:T(8,128)(2,1)}, bf16[512,320]{0,1:T(8,128)(2,1)})) %all-reduce.13.cloned.1.call-update) | async-done | bytes 655376 | tf_op jit(solution)/shard_map/psum | solution.py:106
  698.7 2.8 fusion.22
  701.5 277.2 %all-reduce.11.cloned.1.call-done = f32[512,640]{1,0:T(8,128)} async-done(((f32[512,640]{1,0:T(8,128)}), f32[512,640]{1,0:T(8,128)}) %all-reduce.11.cloned.1.call-update) | async-done | bytes 1310736
  978.7 1.3 fusion.53
  (76 shorter events, 15.5 us)
Async XLA Ops:
  6.5 1.0 copy-start
  7.5 1.6 copy-start.1
  9.1 1.6 copy-start.2
  13.5 50.0 %copy-start.5 = (f32[2,3,640]{2,0,1:T(2,128)S(1)}, f32[2,3,640]{2,0,1:T(2,128)}, u32[]{:S(2)}) copy-start(f32[2,3,640]{2,0,1:T(2,128)} %param.19) | copy-start | bytes 46084
  13.5 50.1 %copy-start.7 = (s32[256,2]{0,1:T(2,128)S(1)}, s32[256,2]{0,1:T(2,128)}, u32[]{:S(2)}) copy-start(s32[256,2]{0,1:T(2,128)} %param.17) | copy-start | bytes 6148
  13.5 50.4 %copy-start.6 = (f32[2,640]{1,0:T(2,128)S(1)}, f32[2,640]{1,0:T(2,128)}, u32[]{:S(2)}) copy-start(f32[2,640]{1,0:T(2,128)} %param.20) | copy-start | bytes 15364
  13.6 42.6 %all-to-all-start.1 = ((bf16[4,64,1,640]{3,0,2,1:T(4,128)(2,1)}), bf16[4,64,1,640]{3,0,2,1:T(4,128)(2,1)S(1)}, u32[]{:S(2)}, u32[]{:S(2)}) async-start(bf16[4,64,1,640]{3,0,2,1:T(4,128)(2,1)} %copy.47), calls=%async_computation.1 | async-start | bytes 655360 | tf_op jit(solution)/shard_map/all_to_all | solution.py:55
  32.4 59.8 %copy-start.8 = (s32[256]{0:T(256)S(1)}, s32[256]{0:T(256)}, u32[]{:S(2)}) copy-start(s32[256]{0:T(256)} %param.18) | copy-start | bytes 3076
  56.1 29.5 %all-to-all-start.2 = ((bf16[4,64,1,640]{3,0,2,1:T(4,128)(2,1)}), bf16[4,64,1,640]{3,0,2,1:T(4,128)(2,1)S(1)}, u32[]{:S(2)}, u32[]{:S(2)}) async-start(bf16[4,64,1,640]{3,0,2,1:T(4,128)(2,1)} %copy.49), calls=%async_computation.2 | async-start | bytes 655360 | tf_op jit(solution)/shard_map/all_to_all | solution.py:56
  85.6 28.9 %all-to-all-start = ((bf16[4,64,1,640]{3,0,2,1:T(4,128)(2,1)}), bf16[4,64,1,640]{3,0,2,1:T(4,128)(2,1)S(1)}, u32[]{:S(2)}, u32[]{:S(2)}) async-start(bf16[4,64,1,640]{3,0,2,1:T(4,128)(2,1)} %copy.46), calls=%async_computation | async-start | bytes 655360 | tf_op jit(solution)/shard_map/all_to_all | solution.py:57
  92.1 206.7 %all-reduce.15.cloned.1.call-start = ((), (), s32[]{:S(2)}) async-start(), calls=%async_computation.7 | async-start | bytes 1310720 | tf_op jit(solution)/shard_map/psum | solution.py:106
  218.1 12.4 %copy-start.3 = (bf16[2,640,320]{1,2,0:T(8,128)(2,1)S(1)}, bf16[2,640,320]{1,2,0:T(8,128)(2,1)}, u32[]{:S(2)}) copy-start(bf16[2,640,320]{1,2,0:T(8,128)(2,1)} %param.22) | copy-start | bytes 2457604
  231.8 347.1 %all-reduce.9.cloned.1.call-start = ((), (), s32[]{:S(2)}) async-start(), calls=%async_computation.4 | async-start | bytes 2621440
  580.6 36.0 %all-to-all-start.3 = ((bf16[64,8,640]{2,1,0:T(8,128)(2,1)}), bf16[64,8,640]{2,1,0:T(8,128)(2,1)S(1)}, u32[]{:S(2)}, u32[]{:S(2)}) async-start(bf16[64,8,640]{2,1,0:T(8,128)(2,1)} %stack.2), calls=%async_computation.3 | async-start | bytes 1310720 | tf_op jit(solution)/shard_map/all_to_all | solution.py:115
  589.8 108.9 %all-reduce.13.cloned.1.call-start = ((), (), s32[]{:S(2)}) async-start(), calls=%async_computation.6 | async-start | bytes 1310720 | tf_op jit(solution)/shard_map/psum | solution.py:106
  628.3 1.3 copy-start.4
  629.6 69.1 %copy-start.9 = (bf16[2,320,640]{2,1,0:T(8,128)(2,1)S(1)}, bf16[2,320,640]{2,1,0:T(8,128)(2,1)}, u32[]{:S(2)}) copy-start(bf16[2,320,640]{2,1,0:T(8,128)(2,1)} %param.23) | copy-start | bytes 2457604
  631.0 347.7 %all-reduce.11.cloned.1.call-start = ((), (), s32[]{:S(2)}) async-start(), calls=%async_computation.5 | async-start | bytes 2621440
Sparse Core Ops, SparseCore 0:
  232.0 66.8 all-reduce.14
  302.2 276.7 all-reduce.8
  631.1 67.5 all-reduce.12
  701.9 276.7 all-reduce.10
